TPU v7x, 512 devices: a whole 4x4x16 slice. The times are simulated.
512 devices in a mesh: depth: 4 (over z_hi, core), plane: 128 (over x, z_lo, y).
Axes of the slice: x: 4, y: 4, z: 16 (z_hi: 2, z_lo: 8; z = z_hi * 8 + z_lo), core: 2. Of those that a mesh axis runs over, the one named last changes fastest.
Arguments:
- magnet: float32 [3, 32, 512, 1024], P(None, 'depth', 'plane'), may hold values from -1 to 1, as said below
- mask: int32 [512, 1024], P('plane'), may hold values 0 or 1
- materials: int32 [32], P('depth'), may hold values from 0 to 3
- exchange_strength: float32 [4], replicated, may hold values from 0.5 to 2
- anisotropy: float32 [4], replicated, may hold values from 0.5 to 3
- damping: float32 [4], replicated, may hold values from 0.05 to 0.6
- source_strength: float32 [4], replicated, may hold values from 0.3 to 1.5
- thermal_strength: float32 [4], replicated, may hold values from 0.5 to 2
- pivots: float32 [32, 3, 3], replicated, may hold values from -1 to 1, as said below
- lower: float32 [32, 3, 3], replicated, may hold values from -1 to 1, as said below
- upper: float32 [32, 3, 3], replicated, may hold values from -1 to 1, as said below
- noise_stream: int32 [1], replicated, may hold values from 0 to 999999
- counter: int32 [1], replicated, may hold values from 0 to 99999
Outputs:
- magnet_next: float32 [3, 32, 512, 1024], P(None, 'depth', 'plane')
- accumulation: float32 [3, 32, 512, 1024], P(None, 'depth', 'plane')
Inputs may be any that keep to these rules, and one draw needn't show every extreme that they name: `magnet`: unit vectors. `pivots`: each block has spectral norm below 0.98. `lower`: each block has spectral norm below 1. `upper`: each block has spectral norm below 1.
All inputs are finite; a program needn't handle non-finite values. No bound on the sum of `mask` on one device may be relied on, other than what follows from the above.
Results may differ from a plain program's by a relative error of at most 0.000073.
Values sent between devices are 32-bit elements; how exact they have to be, the bound alone decides.
A program may use at most 128 MiB of HBM per device.

v0:
```python
import jax
import jax.numpy as jnp
from jax import lax
from jax.sharding import PartitionSpec as P


def padded(block, sides, width, periodic):
    for axis, dim in sides:
        count = lax.axis_size(axis)
        forward = [(i, i + 1) for i in range(count - 1)]
        if periodic:
            forward.append((count - 1, 0))
        backward = [(target, source) for source, target in forward]
        low = lax.ppermute(
            lax.slice_in_dim(block, block.shape[dim] - width, None, axis=dim), axis, forward
        )
        high = lax.ppermute(lax.slice_in_dim(block, 0, width, axis=dim), axis, backward)
        block = jnp.concatenate([low, block, high], axis=dim)
    return block


def cross(a, b):
    return jnp.stack(
        [a[1] * b[2] - a[2] * b[1], a[2] * b[0] - a[0] * b[2], a[0] * b[1] - a[1] * b[0]]
    )


def apply_block(block, vec):
    return jnp.stack(
        [
            block[row, 0] * vec[0] + block[row, 1] * vec[1] + block[row, 2] * vec[2]
            for row in range(3)
        ]
    )


def forward_sweep(source, pivots, lower, initial):
    previous = initial
    values = []
    for layer_pos in range(source.shape[1]):
        previous = apply_block(
            pivots[layer_pos], source[:, layer_pos] - apply_block(lower[layer_pos], previous)
        )
        values.append(previous)
    return values


def backward_sweep(values, upper, initial):
    after = initial
    solved = [None] * len(values)
    for layer_pos in range(len(values) - 1, -1, -1):
        after = values[layer_pos] - apply_block(upper[layer_pos], after)
        solved[layer_pos] = after
    return solved


def solve_columns(source, pivots, lower, upper):
    zero_state = jnp.zeros_like(source[:, 0])
    values = forward_sweep(source, pivots, lower, zero_state)
    return jnp.stack(backward_sweep(values, upper, zero_state), axis=1)


def hash_uniform(index, stream, counter):
    mixed = index * 739982445 + stream * 695872825 + counter * 1597334677
    mixed = mixed ^ lax.shift_right_logical(mixed, jnp.int32(16))
    mixed = mixed * 739982445
    mixed = mixed ^ lax.shift_right_logical(mixed, jnp.int32(15))
    mixed = mixed * 695872825
    mixed = mixed ^ lax.shift_right_logical(mixed, jnp.int32(16))
    return (mixed & 65535).astype(jnp.float32) / 32767.5 - 1.0


def layer_values(materials, table):
    onehot = (materials[:, None] == jnp.arange(table.shape[0], dtype=jnp.int32)[None, :]).astype(
        jnp.float32
    )
    return jnp.sum(onehot * table[None, :], axis=1)[None, :, None, None]


def normalize(vec):
    return vec / jnp.sqrt(jnp.sum(vec * vec, axis=0, keepdims=True))


def spin_solve(source, pivots, lower, upper):
    columns = lax.all_to_all(source, "depth", split_axis=3, concat_axis=1, tiled=True)
    solved = solve_columns(columns, pivots, lower, upper)
    return lax.all_to_all(solved, "depth", split_axis=1, concat_axis=3, tiled=True)


def local(
    magnet,
    mask,
    materials,
    exchange_strength,
    anisotropy,
    damping,
    source_strength,
    thermal_strength,
    pivots,
    lower,
    upper,
    noise_stream,
    counter,
):
    depth_local = magnet.shape[1]
    row_local = magnet.shape[2]
    width_y = magnet.shape[3]
    total_layers = depth_local * lax.axis_size("depth")
    total_rows = row_local * lax.axis_size("plane")
    maskf = mask.astype(jnp.float32)[None, None]
    stiff = layer_values(materials, exchange_strength)
    aniso = layer_values(materials, anisotropy)
    alpha = layer_values(materials, damping)
    beta = layer_values(materials, source_strength)
    theta = layer_values(materials, thermal_strength)
    comp = jnp.arange(3, dtype=jnp.int32)[:, None, None, None]
    layer = (lax.axis_index("depth") * depth_local + jnp.arange(depth_local, dtype=jnp.int32))[
        None, :, None, None
    ]
    xrow = (lax.axis_index("plane") * row_local + jnp.arange(row_local, dtype=jnp.int32))[
        None, None, :, None
    ]
    ycol = jnp.arange(width_y, dtype=jnp.int32)[None, None, None, :]
    index = ((comp * total_layers + layer) * total_rows + xrow) * width_y + ycol
    noise = theta * hash_uniform(index, noise_stream[0], counter[0])
    axis_z = jnp.array([0.0, 0.0, 1.0], dtype=jnp.float32)[:, None, None, None]

    def rate(field):
        masked = field * maskf
        wide = padded(masked, (("plane", 2),), 2, True)
        near = (
            wide[:, :, 3 : row_local + 3]
            + wide[:, :, 1 : row_local + 1]
            + jnp.roll(masked, 1, 3)
            + jnp.roll(masked, -1, 3)
        )
        far = (
            wide[:, :, 4 : row_local + 4]
            + wide[:, :, 0:row_local]
            + jnp.roll(masked, 2, 3)
            + jnp.roll(masked, -2, 3)
        )
        planar = 4.0 / 3.0 * near - 1.0 / 12.0 * far
        stacked = padded(masked, (("depth", 1),), 1, False)
        vertical = stacked[:, 2:] + stacked[:, :-2]
        accum = spin_solve(beta * field, pivots, lower, upper)
        heff = stiff * (planar + 0.5 * vertical) + aniso * field * axis_z + noise + 0.5 * accum
        torque = cross(field, heff)
        change = -(torque + alpha * cross(field, torque)) / (1.0 + alpha * alpha) * maskf
        return (change, accum)

    first, _ = rate(magnet)
    middle = normalize(magnet + 0.03 * first)
    second, accum = rate(middle)
    magnet_next = normalize(magnet + 0.015 * (first + second))
    return (magnet_next, accum)


def solution(mesh):
    placed = (
        P(None, "depth", "plane", None),
        P("plane", None),
        P("depth"),
        P(),
        P(),
        P(),
        P(),
        P(),
        P(),
        P(),
        P(),
        P(),
        P(),
    )
    return jax.shard_map(
        local,
        mesh=mesh,
        in_specs=placed,
        out_specs=(P(None, "depth", "plane", None), P(None, "depth", "plane", None)),
        check_vma=False,
    )
```

profile of v0, /device:TPU:3, one launch (start us, length us, event | category | flops | bytes accessed | tf_op | source)
XLA Modules:
  0.0 1313.8 jit_solution(13437907100284906902)
XLA Ops:
  8.7 9.2 reshape.5395
  17.9 15.8 %all-to-all-start = ((f32[4,1,24576]{2,1,0:T(1,128)}), f32[4,1,24576]{2,1,0:T(1,128)S(1)}, u32[]{:S(2)}, u32[]{:S(2)}) async-start(f32[4,1,24576]{2,1,0:T(1,128)} %reshape.5395), calls=%async_computation | async-start | bytes 786432 | tf_op jit(solution)/shard_map/all_to_all | solution.py:85
  34.4 7.8 collective-permute-start
  47.0 12.7 collective-permute-start.3
  113.4 10.3 reshape.5396
  129.2 7.5 multiply_add_fusion.555
  163.0 7.5 multiply_add_fusion.537
  174.2 7.6 multiply_add_fusion.531
  185.8 7.6 multiply_add_fusion.525
  197.2 7.8 multiply_add_fusion.519
  220.0 7.6 multiply_add_fusion.507
  231.3 7.6 multiply_add_fusion.501
  254.0 7.6 multiply_add_fusion.489
  265.4 7.6 multiply_add_fusion.483
  276.6 7.5 multiply_add_fusion.477
  287.9 7.6 multiply_add_fusion.471
  332.8 7.6 multiply_add_fusion.447
  355.2 7.5 multiply_add_fusion.435
  366.5 7.6 multiply_add_fusion.429
  400.2 7.5 multiply_add_fusion.411
  411.6 7.6 multiply_add_fusion.405
  423.0 7.5 multiply_add_fusion.399
  445.3 7.5 multiply_add_fusion.387
  456.7 7.5 multiply_add_fusion.381
  664.1 19.8 %all-to-all-done.1 = f32[3,32,4,256]{3,2,0,1:T(4,128)S(1)} async-done(((f32[3,32,4,256]{3,2,0,1:T(4,128)}), f32[3,32,4,256]{3,2,0,1:T(4,128)S(1)}, u32[]{:S(2)}, u32[]{:S(2)}) %all-to-all-start.1) | async-done | bytes 393248 | tf_op jit(solution)/shard_map/all_to_all | solution.py:87
  691.3 9.2 reshape.5397
  705.5 17.5 %collective-permute-start.4 = (f32[3,8,2,1024]{3,1,2,0:T(8,128)}, f32[3,8,2,1024]{3,1,2,0:T(8,128)}, u32[]{:S(2)}, u32[]{:S(2)}) collective-permute-start(f32[3,8,2,1024]{3,1,2,0:T(8,128)} %get-tuple-element.415), channel_id=1, source_target_pairs={{1,0},{2,1},{3,2},{4,3},{5,4},{6,5},{7,6},{8,7},{9,8},{10,9},{11,1... | collective-permute-start | bytes 589832 | tf_op jit(solution)/shard_map/ppermute | solution.py:17
  726.9 10.3 reshape.5398
  742.6 7.5 multiply_add_fusion.276
  776.3 7.5 multiply_add_fusion.258
  787.5 7.6 multiply_add_fusion.252
  799.2 7.6 multiply_add_fusion.246
  810.6 7.8 multiply_add_fusion.240
  833.4 7.6 multiply_add_fusion.228
  844.7 7.6 multiply_add_fusion.222
  867.3 7.6 multiply_add_fusion.210
  878.7 7.6 multiply_add_fusion.204
  889.9 7.5 multiply_add_fusion.198
  901.2 7.6 multiply_add_fusion.192
  946.2 7.6 multiply_add_fusion.168
  968.5 7.5 multiply_add_fusion.156
  979.8 7.6 multiply_add_fusion.150
  1013.5 7.5 multiply_add_fusion.132
  1024.8 7.6 multiply_add_fusion.126
  1036.3 7.5 multiply_add_fusion.120
  1058.6 7.5 multiply_add_fusion.108
  1272.9 12.3 all-to-all-start.3
  1287.8 12.4 collective-permute-start.7
  (500 shorter events, 879.9 us)
Async XLA Ops:
  2.7 1.3 copy-start.6
  2.8 660.3 %copy-start.10 = (f32[8]{0:T(128)}, f32[8]{0:T(128)S(1)}, u32[]{:S(2)}) copy-start(f32[8]{0:T(128)S(1)} %get-tuple-element.104) | copy-start | bytes 100
  4.0 55.7 %copy-start.1 = (f32[32,3,3]{0,2,1:T(4,128)S(1)}, f32[32,3,3]{0,2,1:T(4,128)}, u32[]{:S(2)}) copy-start(f32[32,3,3]{0,2,1:T(4,128)} %param.23) | copy-start | bytes 3460
  4.0 56.2 %copy-start.2 = (f32[32,3,3]{0,2,1:T(4,128)S(1)}, f32[32,3,3]{0,2,1:T(4,128)}, u32[]{:S(2)}) copy-start(f32[32,3,3]{0,2,1:T(4,128)} %param.22) | copy-start | bytes 3460
  4.0 56.7 %copy-start.3 = (f32[32,3,3]{0,2,1:T(4,128)S(1)}, f32[32,3,3]{0,2,1:T(4,128)}, u32[]{:S(2)}) copy-start(f32[32,3,3]{0,2,1:T(4,128)} %param.24) | copy-start | bytes 3460
  17.9 93.2 %all-to-all-start = ((f32[4,1,24576]{2,1,0:T(1,128)}), f32[4,1,24576]{2,1,0:T(1,128)S(1)}, u32[]{:S(2)}, u32[]{:S(2)}) async-start(f32[4,1,24576]{2,1,0:T(1,128)} %reshape.5395), calls=%async_computation | async-start | bytes 786432 | tf_op jit(solution)/shard_map/all_to_all | solution.py:85
  34.4 649.6 %collective-permute-start = (f32[3,8,2,1024]{3,1,2,0:T(8,128)}, f32[3,8,2,1024]{3,1,2,0:T(8,128)S(1)}, u32[]{:S(2)}, u32[]{:S(2)}) collective-permute-start(f32[3,8,2,1024]{3,1,2,0:T(8,128)} %get-tuple-element.427), channel_id=1, source_target_pairs={{1,0},{2,1},{3,2},{4,3},{5,4},{6,5},{7,6},{8,7},{9,8},{10,9},{11,1... | collective-permute-start | bytes 589832 | tf_op jit(solution)/shard_map/ppermute | solution.py:17
  42.2 641.8 %collective-permute-start.1 = (f32[3,8,2,1024]{3,1,2,0:T(8,128)}, f32[3,8,2,1024]{3,1,2,0:T(8,128)}, u32[]{:S(2)}, u32[]{:S(2)}) collective-permute-start(f32[3,8,2,1024]{3,1,2,0:T(8,128)} %get-tuple-element.428), channel_id=1, source_target_pairs={{0,1},{1,2},{2,3},{3,4},{4,5},{5,6},{6,7},{7,8},{8,9},{9,10},{10,1... | collective-permute-start | bytes 589832 | tf_op jit(solution)/shard_map/ppermute | solution.py:14
  44.8 639.1 %collective-permute-start.2 = (f32[3,1,4,1024]{3,1,2,0:T(1,128)}, f32[3,1,4,1024]{3,1,2,0:T(1,128)}, u32[]{:S(2)}, u32[]{:S(2)}) collective-permute-start(f32[3,1,4,1024]{3,1,2,0:T(1,128)} %get-tuple-element.425), channel_id=1, source_target_pairs={{128,0},{256,128},{384,256},{129,1},{257,129},{385,257},{130,2},{2... | collective-permute-start | bytes 147464 | tf_op jit(solution)/shard_map/ppermute | solution.py:17
  47.0 636.9 %collective-permute-start.3 = (f32[3,1,4,1024]{3,1,2,0:T(1,128)}, f32[3,1,4,1024]{3,1,2,0:T(1,128)}, u32[]{:S(2)}, u32[]{:S(2)}) collective-permute-start(f32[3,1,4,1024]{3,1,2,0:T(1,128)} %get-tuple-element.426), channel_id=1, source_target_pairs={{0,128},{128,256},{256,384},{1,129},{129,257},{257,385},{2,130},{1... | collective-permute-start | bytes 147464 | tf_op jit(solution)/shard_map/ppermute | solution.py:14
  104.6 24.5 %copy-start.8 = (f32[3]{0:T(128)}, f32[3]{0:T(128)S(1)}, u32[]{:S(2)}) copy-start(f32[3]{0:T(128)S(1)} %maximum_maximum_fusion.1) | copy-start | bytes 40
  104.7 554.0 %copy-start.4 = (f32[3]{0:T(128)}, f32[3]{0:T(128)S(1)}, u32[]{:S(2)}) copy-start(f32[3]{0:T(128)S(1)} %maximum_maximum_fusion) | copy-start | bytes 40
  366.4 317.6 %copy-start = (f32[3,8,4,1024]{3,2,1,0:T(4,128)S(1)}, f32[3,8,4,1024]{3,2,1,0:T(4,128)}, u32[]{:S(2)}) copy-start(f32[3,8,4,1024]{3,2,1,0:T(4,128)} %param.14) | copy-start | bytes 1179652
  659.6 24.3 %all-to-all-start.1 = ((f32[3,32,4,256]{3,2,0,1:T(4,128)}), f32[3,32,4,256]{3,2,0,1:T(4,128)S(1)}, u32[]{:S(2)}, u32[]{:S(2)}) async-start(f32[3,32,4,256]{3,2,0,1:T(4,128)} %copy.279), calls=%async_computation.1 | async-start | bytes 786432 | tf_op jit(solution)/shard_map/all_to_all | solution.py:87
  683.9 2.1 copy-start.11
  683.9 2.1 copy-start.13
  683.9 2.5 copy-start.7
  700.5 24.6 %all-to-all-start.2 = ((f32[4,1,24576]{2,1,0:T(1,128)}), f32[4,1,24576]{2,1,0:T(1,128)S(1)}, u32[]{:S(2)}, u32[]{:S(2)}) async-start(f32[4,1,24576]{2,1,0:T(1,128)} %reshape.5397), calls=%async_computation.2 | async-start | bytes 786432 | tf_op jit(solution)/shard_map/all_to_all | solution.py:85
  705.5 604.6 %collective-permute-start.4 = (f32[3,8,2,1024]{3,1,2,0:T(8,128)}, f32[3,8,2,1024]{3,1,2,0:T(8,128)}, u32[]{:S(2)}, u32[]{:S(2)}) collective-permute-start(f32[3,8,2,1024]{3,1,2,0:T(8,128)} %get-tuple-element.415), channel_id=1, source_target_pairs={{1,0},{2,1},{3,2},{4,3},{5,4},{6,5},{7,6},{8,7},{9,8},{10,9},{11,1... | collective-permute-start | bytes 589832 | tf_op jit(solution)/shard_map/ppermute | solution.py:17
  723.0 587.1 %collective-permute-start.5 = (f32[3,8,2,1024]{3,1,2,0:T(8,128)}, f32[3,8,2,1024]{3,1,2,0:T(8,128)}, u32[]{:S(2)}, u32[]{:S(2)}) collective-permute-start(f32[3,8,2,1024]{3,1,2,0:T(8,128)} %get-tuple-element.416), channel_id=1, source_target_pairs={{0,1},{1,2},{2,3},{3,4},{4,5},{5,6},{6,7},{7,8},{8,9},{9,10},{10,1... | collective-permute-start | bytes 589832 | tf_op jit(solution)/shard_map/ppermute | solution.py:14
  726.9 15.6 %copy-start.9 = (f32[3]{0:T(128)S(1)}, f32[3]{0:T(128)}, u32[]{:S(2)}) copy-start(f32[3]{0:T(128)} %copy-done.8) | copy-start | bytes 40
  737.1 360.8 %copy-start.5 = (f32[3]{0:T(128)S(1)}, f32[3]{0:T(128)}, u32[]{:S(2)}) copy-start(f32[3]{0:T(128)} %copy-done.4) | copy-start | bytes 40
  1272.9 29.0 %all-to-all-start.3 = ((f32[3,32,4,256]{3,2,0,1:T(4,128)}), f32[3,32,4,256]{3,2,0,1:T(4,128)S(1)}, u32[]{:S(2)}, u32[]{:S(2)}) async-start(f32[3,32,4,256]{3,2,0,1:T(4,128)} %copy.319), calls=%async_computation.3 | async-start | bytes 786432 | tf_op jit(solution)/shard_map/all_to_all | solution.py:87
  1285.9 24.2 %collective-permute-start.6 = (f32[3,1,4,1024]{3,1,2,0:T(1,128)}, f32[3,1,4,1024]{3,1,2,0:T(1,128)}, u32[]{:S(2)}, u32[]{:S(2)}) collective-permute-start(f32[3,1,4,1024]{3,1,2,0:T(1,128)} %get-tuple-element.413), channel_id=1, source_target_pairs={{128,0},{256,128},{384,256},{129,1},{257,129},{385,257},{130,2},{2... | collective-permute-start | bytes 147464 | tf_op jit(solution)/shard_map/ppermute | solution.py:17
  1287.8 22.3 %collective-permute-start.7 = (f32[3,1,4,1024]{3,1,2,0:T(1,128)}, f32[3,1,4,1024]{3,1,2,0:T(1,128)}, u32[]{:S(2)}, u32[]{:S(2)}) collective-permute-start(f32[3,1,4,1024]{3,1,2,0:T(1,128)} %get-tuple-element.414), channel_id=1, source_target_pairs={{0,128},{128,256},{256,384},{1,129},{129,257},{257,385},{2,130},{1... | collective-permute-start | bytes 147464 | tf_op jit(solution)/shard_map/ppermute | solution.py:14
  1301.9 10.2 copy-start.12
  1301.9 10.2 copy-start.14
where the time goes:
time: 1330 us; the launch traced here: 1310 us
  other arithmetic  1070 us (80%)
  local copies, waits for them, and re-layouts  106 us (8%)
  starting transfers between devices  94.2 us (7%)
  waiting for transfers between devices  26.9 us (2%)
  between operations  16.5 us (1%)
    add x186, other arithmetic, apply_block(): block[row, 0] * vec[0] + block[row, 1] * vec[1] + block[row, 2] * vec[2]  1040 us
    unnamed x36, local copies, waits for them, and re-layouts  41 us
    slice x49, local copies, waits for them, and re-layouts, apply_block(): block[row, 0] * vec[0] + block[row, 1] * vec[1] + block[row, 2] * vec[2]  34.9 us
    ppermute x4, starting transfers between devices, padded(): lax.ppermute(lax.slice_in_dim(block, 0, width, axis=dim), axis, backward)  29.4 us
    ppermute x4, starting transfers between devices, padded(): lax.ppermute(lax.slice_in_dim(block, block.shape[dim] - width, None, axis...  29.1 us
  transfers between devices with their start and end apart: 12, of which 2 were waited for; matrix products, arithmetic and copies ran while one was open for 87% of the time, Pallas kernels for 0%

commit v1 on v0

--- a/solution.py
+++ b/solution.py
@@ -2,6 +2,7 @@
 import jax.numpy as jnp
 from jax import lax
 from jax.sharding import PartitionSpec as P
+from jax.lax import all_to_all, axis_size
 
 
 def padded(block, sides, width, periodic):
@@ -82,7 +83,15 @@
 
 
 def spin_solve(source, pivots, lower, upper):
-    columns = lax.all_to_all(source, "depth", split_axis=3, concat_axis=1, tiled=True)
+    columns = jnp.concatenate(
+        all_to_all(
+            jnp.stack(jnp.split(source, axis_size("depth"), 3)),
+            "depth",
+            split_axis=0,
+            concat_axis=0,
+        ),
+        1,
+    )
     solved = solve_columns(columns, pivots, lower, upper)
     return lax.all_to_all(solved, "depth", split_axis=1, concat_axis=3, tiled=True)
 

time: 1330 us -> 1270 us (0.955)
  local copies, waits for them, and re-layouts: 106 us -> 52.9 us
    unnamed x36 -> x72, local copies, waits for them, and re-layouts: 41 us -> 7.87 us
  transfers between devices with their start and end apart: 12 -> 12, of which waited for: 2 -> 2; matrix products, arithmetic and copies ran while one was open for 87% -> 88% of each run, Pallas kernels for 0% -> 0%
where the time goes in v1:
time: 1270 us; the launch traced here: 1260 us
  other arithmetic  1070 us (84%)
  starting transfers between devices  93.7 us (7%)
  local copies, waits for them, and re-layouts  52.9 us (4%)
  waiting for transfers between devices  26.9 us (2%)
  between operations  16.8 us (1%)
    add x186, other arithmetic, apply_block(): block[row, 0] * vec[0] + block[row, 1] * vec[1] + block[row, 2] * vec[2]  1040 us
    slice x49, local copies, waits for them, and re-layouts, apply_block(): block[row, 0] * vec[0] + block[row, 1] * vec[1] + block[row, 2] * vec[2]  34.6 us
    ppermute x4, starting transfers between devices, padded(): lax.ppermute(lax.slice_in_dim(block, 0, width, axis=dim), axis, backward)  29.4 us
    ppermute x4, starting transfers between devices, padded(): lax.ppermute(lax.slice_in_dim(block, block.shape[dim] - width, None, axis...  28.5 us
  transfers between devices with their start and end apart: 12, of which 2 were waited for; matrix products, arithmetic and copies ran while one was open for 88% of the time, Pallas kernels for 0%

profile of v1, /device:TPU:3, one launch (start us, length us, event | category | flops | bytes accessed | tf_op | source)
XLA Modules:
  0.0 1256.7 jit_solution(18408663036213584316)
XLA Ops:
  4.8 15.8 %all-to-all-start = ((f32[4,3,8,4,256]{4,2,3,1,0:T(8,128)}), f32[4,3,8,4,256]{4,2,3,1,0:T(8,128)S(1)}, u32[]{:S(2)}, u32[]{:S(2)}) async-start(f32[4,3,8,4,256]{4,2,3,1,0:T(8,128)} %pad_maximum_fusion.8), calls=%async_computation | async-start | bytes 786432 | tf_op jit(solution)/shard_map/all_to_all | solution.py:87
  21.4 7.8 collective-permute-start
  34.0 12.3 collective-permute-start.3
  98.8 7.5 multiply_add_fusion.555
  121.2 7.5 multiply_add_fusion.543
  132.5 7.5 multiply_add_fusion.537
  143.7 7.5 multiply_add_fusion.531
  154.8 7.4 multiply_add_fusion.525
  166.0 7.5 multiply_add_fusion.519
  188.2 7.4 multiply_add_fusion.507
  199.5 7.5 multiply_add_fusion.501
  210.8 7.6 multiply_add_fusion.495
  222.3 7.4 multiply_add_fusion.489
  277.8 7.4 multiply_add_fusion.459
  288.9 7.4 multiply_add_fusion.453
  311.2 7.6 multiply_add_fusion.441
  344.7 7.6 multiply_add_fusion.423
  356.0 7.6 multiply_add_fusion.417
  367.3 7.5 multiply_add_fusion.411
  378.6 7.7 multiply_add_fusion.405
  390.2 7.5 multiply_add_fusion.399
  401.6 7.6 multiply_add_fusion.393
  423.7 7.7 multiply_add_fusion.381
  435.2 7.7 multiply_add_fusion.375
  633.4 19.6 %all-to-all-done.1 = f32[3,32,4,256]{3,2,0,1:T(4,128)S(1)} async-done(((f32[3,32,4,256]{3,2,0,1:T(4,128)}), f32[3,32,4,256]{3,2,0,1:T(4,128)S(1)}, u32[]{:S(2)}, u32[]{:S(2)}) %all-to-all-start.1) | async-done | bytes 393248 | tf_op jit(solution)/shard_map/all_to_all | solution.py:96
  663.5 17.5 %collective-permute-start.4 = (f32[3,8,2,1024]{3,1,2,0:T(8,128)}, f32[3,8,2,1024]{3,1,2,0:T(8,128)}, u32[]{:S(2)}, u32[]{:S(2)}) collective-permute-start(f32[3,8,2,1024]{3,1,2,0:T(8,128)} %get-tuple-element.421), channel_id=1, source_target_pairs={{1,0},{2,1},{3,2},{4,3},{5,4},{6,5},{7,6},{8,7},{9,8},{10,9},{11,1... | collective-permute-start | bytes 589832 | tf_op jit(solution)/shard_map/ppermute | solution.py:18
  684.0 7.5 multiply_add_fusion.276
  706.4 7.5 multiply_add_fusion.264
  717.6 7.5 multiply_add_fusion.258
  728.9 7.5 multiply_add_fusion.252
  751.1 7.5 multiply_add_fusion.240
  773.3 7.4 multiply_add_fusion.228
  784.6 7.5 multiply_add_fusion.222
  796.0 7.6 multiply_add_fusion.216
  807.5 7.4 multiply_add_fusion.210
  863.0 7.4 multiply_add_fusion.180
  874.0 7.4 multiply_add_fusion.174
  896.4 7.6 multiply_add_fusion.162
  929.8 7.6 multiply_add_fusion.144
  941.1 7.6 multiply_add_fusion.138
  952.5 7.5 multiply_add_fusion.132
  963.7 7.7 multiply_add_fusion.126
  975.3 7.5 multiply_add_fusion.120
  986.7 7.6 multiply_add_fusion.114
  1008.9 7.7 multiply_add_fusion.102
  1020.3 7.7 multiply_add_fusion.96
  1214.5 12.3 all-to-all-start.3
  1229.4 12.4 collective-permute-start.7
  (535 shorter events, 833.4 us)
Async XLA Ops:
  0.6 0.8 copy-start.30
  0.6 0.8 copy-start.34
  0.7 0.8 copy-start.33
  0.7 0.8 copy-start.29
  0.7 0.8 copy-start.31
  0.7 0.8 copy-start.32
  2.2 0.6 copy-start.12
  2.2 630.2 %copy-start.22 = (f32[8]{0:T(128)}, f32[8]{0:T(128)S(1)}, u32[]{:S(2)}) copy-start(f32[8]{0:T(128)S(1)} %get-tuple-element.106) | copy-start | bytes 100
  4.8 93.6 %all-to-all-start = ((f32[4,3,8,4,256]{4,2,3,1,0:T(8,128)}), f32[4,3,8,4,256]{4,2,3,1,0:T(8,128)S(1)}, u32[]{:S(2)}, u32[]{:S(2)}) async-start(f32[4,3,8,4,256]{4,2,3,1,0:T(8,128)} %pad_maximum_fusion.8), calls=%async_computation | async-start | bytes 786432 | tf_op jit(solution)/shard_map/all_to_all | solution.py:87
  21.4 631.8 %collective-permute-start = (f32[3,8,2,1024]{3,1,2,0:T(8,128)}, f32[3,8,2,1024]{3,1,2,0:T(8,128)S(1)}, u32[]{:S(2)}, u32[]{:S(2)}) collective-permute-start(f32[3,8,2,1024]{3,1,2,0:T(8,128)} %get-tuple-element.433), channel_id=1, source_target_pairs={{1,0},{2,1},{3,2},{4,3},{5,4},{6,5},{7,6},{8,7},{9,8},{10,9},{11,1... | collective-permute-start | bytes 589832 | tf_op jit(solution)/shard_map/ppermute | solution.py:18
  29.2 624.0 %collective-permute-start.1 = (f32[3,8,2,1024]{3,1,2,0:T(8,128)}, f32[3,8,2,1024]{3,1,2,0:T(8,128)}, u32[]{:S(2)}, u32[]{:S(2)}) collective-permute-start(f32[3,8,2,1024]{3,1,2,0:T(8,128)} %get-tuple-element.434), channel_id=1, source_target_pairs={{0,1},{1,2},{2,3},{3,4},{4,5},{5,6},{6,7},{7,8},{8,9},{9,10},{10,1... | collective-permute-start | bytes 589832 | tf_op jit(solution)/shard_map/ppermute | solution.py:15
  31.1 15.2 %copy-start.1 = (f32[32,3,3]{0,2,1:T(4,128)S(1)}, f32[32,3,3]{0,2,1:T(4,128)}, u32[]{:S(2)}) copy-start(f32[32,3,3]{0,2,1:T(4,128)} %param.23) | copy-start | bytes 3460
  31.8 621.3 %collective-permute-start.2 = (f32[3,1,4,1024]{3,1,2,0:T(1,128)}, f32[3,1,4,1024]{3,1,2,0:T(1,128)}, u32[]{:S(2)}, u32[]{:S(2)}) collective-permute-start(f32[3,1,4,1024]{3,1,2,0:T(1,128)} %get-tuple-element.431), channel_id=1, source_target_pairs={{128,0},{256,128},{384,256},{129,1},{257,129},{385,257},{130,2},{2... | collective-permute-start | bytes 147464 | tf_op jit(solution)/shard_map/ppermute | solution.py:18
  34.0 619.1 %collective-permute-start.3 = (f32[3,1,4,1024]{3,1,2,0:T(1,128)}, f32[3,1,4,1024]{3,1,2,0:T(1,128)}, u32[]{:S(2)}, u32[]{:S(2)}) collective-permute-start(f32[3,1,4,1024]{3,1,2,0:T(1,128)} %get-tuple-element.432), channel_id=1, source_target_pairs={{0,128},{128,256},{256,384},{1,129},{129,257},{257,385},{2,130},{1... | collective-permute-start | bytes 147464 | tf_op jit(solution)/shard_map/ppermute | solution.py:15
  46.5 0.7 copy-start.2
  47.4 0.7 copy-start.3
  92.0 6.8 copy-start.20
  92.1 535.8 %copy-start.10 = (f32[3]{0:T(128)}, f32[3]{0:T(128)S(1)}, u32[]{:S(2)}) copy-start(f32[3]{0:T(128)S(1)} %maximum_maximum_fusion) | copy-start | bytes 40
  628.7 24.3 %all-to-all-start.1 = ((f32[3,32,4,256]{3,2,0,1:T(4,128)}), f32[3,32,4,256]{3,2,0,1:T(4,128)S(1)}, u32[]{:S(2)}, u32[]{:S(2)}) async-start(f32[3,32,4,256]{3,2,0,1:T(4,128)} %copy.291), calls=%async_computation.1 | async-start | bytes 786432 | tf_op jit(solution)/shard_map/all_to_all | solution.py:96
  633.4 19.8 %copy-start = (f32[3,8,4,1024]{3,2,1,0:T(4,128)S(1)}, f32[3,8,4,1024]{3,2,1,0:T(4,128)}, u32[]{:S(2)}) copy-start(f32[3,8,4,1024]{3,2,1,0:T(4,128)} %param.14) | copy-start | bytes 1179652
  653.2 0.7 copy-start.8
  653.2 0.7 copy-start.25
  653.2 0.7 copy-start.14
  653.2 0.7 copy-start.16
  653.2 0.7 copy-start.18
  655.8 0.6 copy-start.23
  655.8 0.6 copy-start.27
  656.8 0.7 copy-start.13
  658.6 24.4 %all-to-all-start.2 = ((f32[4,3,8,4,256]{4,2,3,1,0:T(8,128)}), f32[4,3,8,4,256]{4,2,3,1,0:T(8,128)S(1)}, u32[]{:S(2)}, u32[]{:S(2)}) async-start(f32[4,3,8,4,256]{4,2,3,1,0:T(8,128)} %pad_maximum_fusion.9), calls=%async_computation.2 | async-start | bytes 786432 | tf_op jit(solution)/shard_map/all_to_all | solution.py:87
  663.5 588.5 %collective-permute-start.4 = (f32[3,8,2,1024]{3,1,2,0:T(8,128)}, f32[3,8,2,1024]{3,1,2,0:T(8,128)}, u32[]{:S(2)}, u32[]{:S(2)}) collective-permute-start(f32[3,8,2,1024]{3,1,2,0:T(8,128)} %get-tuple-element.421), channel_id=1, source_target_pairs={{1,0},{2,1},{3,2},{4,3},{5,4},{6,5},{7,6},{8,7},{9,8},{10,9},{11,1... | collective-permute-start | bytes 589832 | tf_op jit(solution)/shard_map/ppermute | solution.py:18
  681.0 570.9 %collective-permute-start.5 = (f32[3,8,2,1024]{3,1,2,0:T(8,128)}, f32[3,8,2,1024]{3,1,2,0:T(8,128)}, u32[]{:S(2)}, u32[]{:S(2)}) collective-permute-start(f32[3,8,2,1024]{3,1,2,0:T(8,128)} %get-tuple-element.422), channel_id=1, source_target_pairs={{0,1},{1,2},{2,3},{3,4},{4,5},{5,6},{6,7},{7,8},{8,9},{9,10},{10,1... | collective-permute-start | bytes 589832 | tf_op jit(solution)/shard_map/ppermute | solution.py:15
  683.3 0.6 copy-start.21
  1037.6 0.7 copy-start.11
  1214.5 29.0 %all-to-all-start.3 = ((f32[3,32,4,256]{3,2,0,1:T(4,128)}), f32[3,32,4,256]{3,2,0,1:T(4,128)S(1)}, u32[]{:S(2)}, u32[]{:S(2)}) async-start(f32[3,32,4,256]{3,2,0,1:T(4,128)} %copy.329), calls=%async_computation.3 | async-start | bytes 786432 | tf_op jit(solution)/shard_map/all_to_all | solution.py:96
  1227.5 24.4 %collective-permute-start.6 = (f32[3,1,4,1024]{3,1,2,0:T(1,128)}, f32[3,1,4,1024]{3,1,2,0:T(1,128)}, u32[]{:S(2)}, u32[]{:S(2)}) collective-permute-start(f32[3,1,4,1024]{3,1,2,0:T(1,128)} %get-tuple-element.419), channel_id=1, source_target_pairs={{128,0},{256,128},{384,256},{129,1},{257,129},{385,257},{130,2},{2... | collective-permute-start | bytes 147464 | tf_op jit(solution)/shard_map/ppermute | solution.py:18
  1229.4 22.5 %collective-permute-start.7 = (f32[3,1,4,1024]{3,1,2,0:T(1,128)}, f32[3,1,4,1024]{3,1,2,0:T(1,128)}, u32[]{:S(2)}, u32[]{:S(2)}) collective-permute-start(f32[3,1,4,1024]{3,1,2,0:T(1,128)} %get-tuple-element.420), channel_id=1, source_target_pairs={{0,128},{128,256},{256,384},{1,129},{129,257},{257,385},{2,130},{1... | collective-permute-start | bytes 147464 | tf_op jit(solution)/shard_map/ppermute | solution.py:15
  1243.7 8.4 copy-start.4
  1243.7 8.4 copy-start.5
  1243.7 8.4 copy-start.6
  1243.7 8.4 copy-start.7
  1243.7 8.4 copy-start.26
  1252.0 0.7 copy-start.9
  1252.0 0.7 copy-start.15
  1252.0 0.7 copy-start.17
  1252.0 0.7 copy-start.19
  1254.7 0.6 copy-start.24
  1254.7 0.6 copy-start.28
